TPU v7x, 32 devices: a whole 2x2x4 slice. The times are simulated.
32 devices in a mesh: section: 4 (over y, core), chan: 8 (over z, x).
Axes of the slice: x: 2, y: 2, z: 4, core: 2. Of those that a mesh axis runs over, the one named last changes fastest.
Arguments:
- raw_traces: bfloat16 [2048, 1024], P(('section', 'chan')), may hold values from -6 to 6
- fir_taps: bfloat16 [64], replicated, may hold values from -0.75 to 0.75
- space_taps: float32 [33], replicated, may hold values from -1 to 1
- source_index: int32 [4, 96], P('section', 'chan'), may hold values from 0 to 511, as said below
Outputs:
- gathers: bfloat16 [2048, 64, 96], P(('section', 'chan'))
Inputs may be any that keep to these rules, and one draw needn't show every extreme that they name: `source_index`: entries j * 12 to (j + 1) * 12 - 1 of a section's row are distinct and lie in channels j * 64 to (j + 1) * 64 - 1; the first such block of every section names channel 0 and the last names channel 512 - 1.
All inputs are finite; a program needn't handle non-finite values.
Results may differ from a plain program's by a relative error of at most 0.0058.
Values may be sent and summed in bfloat16 or wider, within the bound.
A program may use at most 64 MiB of HBM per device.

v0:
```python
import jax
import jax.numpy as jnp
from jax import lax
from jax.sharding import PartitionSpec as P

LAGS = 64


def extended(x, sides, width):
    for axis, dim in sides:
        size, length = (lax.axis_size(axis), x.shape[dim])
        up = [(i, (i + 1) % size) for i in range(size - 1)]
        down = [(j, i) for i, j in up]
        last = lax.slice_in_dim(x, length - width, length, axis=dim)
        leading = lax.slice_in_dim(x, 0, width, axis=dim)
        before = lax.ppermute(last, axis, up)
        after = lax.ppermute(leading, axis, down)
        x = jnp.concatenate([before, x, after], axis=dim)
    return x


def fir_matrix(taps, length):
    count = taps.shape[0]
    lead = jnp.zeros((length - 1,), taps.dtype)
    tail = jnp.zeros((length + 1 - count,), taps.dtype)
    period = jnp.concatenate([lead, taps, tail])
    flat = jnp.tile(period, length)[: length * (2 * length - 1)]
    return flat.reshape(length, 2 * length - 1)[:, length - 1 :]


def space_filter(padded, space_taps, rows):
    total = jnp.zeros((rows, padded.shape[1]), jnp.float32)
    for offset in range(space_taps.shape[0]):
        total = total + space_taps[offset] * padded[offset : offset + rows].astype(jnp.float32)
    return total.astype(jnp.bfloat16)


def correlate(receivers, sources):
    rows, length = receivers.shape
    blocks = []
    for first in range(0, LAGS, 8):
        shifted = []
        for lag in range(first, first + 8):
            shifted.append(jnp.pad(receivers[:, lag:], ((0, 0), (0, lag))))
        stacked = jnp.stack(shifted, axis=1).reshape(rows * 8, length)
        block = lax.dot_general(
            stacked, sources, (((1,), (1,)), ((), ())), preferred_element_type=jnp.float32
        )
        blocks.append(block.reshape(rows, 8, sources.shape[0]))
    joined = jnp.concatenate(blocks, axis=1)
    return (joined * (1.0 / length**0.5)).astype(jnp.bfloat16)


def shards(raw_traces, fir_taps, space_taps, source_index):
    rows, length = raw_traces.shape
    banded = jnp.dot(
        raw_traces, fir_matrix(fir_taps, length), preferred_element_type=jnp.float32
    ).astype(jnp.bfloat16)
    half = (space_taps.shape[0] - 1) // 2
    padded = extended(banded, ((("section", "chan"), 0),), half)
    filtered = space_filter(padded, space_taps, rows)
    whole_traces, whole_index = (
        lax.all_gather(filtered, "chan", axis=0, tiled=True),
        lax.all_gather(source_index, "chan", axis=1, tiled=True),
    )
    sources = jnp.take(whole_traces, whole_index[0], axis=0)
    return correlate(filtered, sources)


def solution(mesh):
    return jax.shard_map(
        shards,
        mesh=mesh,
        in_specs=(P(("section", "chan"), None), P(), P(), P("section", "chan")),
        out_specs=P(("section", "chan"), None, None),
        check_vma=False,
    )
```

profile of v0, /device:TPU:0, one launch (start us, length us, event | category | flops | bytes accessed | tf_op | source)
XLA Modules:
  0.0 132.3 jit_solution(16714103273075158136)
XLA Ops:
  6.5 0.8 concatenate.43
  7.3 1.0 broadcast_bitcast_fusion
  8.4 1.4 %copy.29 = bf16[128,16,8,128]{3,1,2,0:T(8,128)(2,1)S(1)} copy(bf16[128,16,8,128]{3,2,1,0:T(8,128)(2,1)S(1)} %broadcast_bitcast_fusion) | data formatting | bytes 8388608
  9.8 2.2 %slice.562 = bf16[2096128]{0:T(1024)(128)(2,1)} slice(bf16[2097152]{0:T(1024)(128)(2,1)S(1)} %bitcast.199), slice={[0:2096128]} | slice | bytes 8384512 | tf_op jit(solution)/shard_map/slice | solution.py:27
  12.0 10.7 %reshape.70 = bf16[1024,2047]{1,0:T(8,128)(2,1)} reshape(bf16[2096128]{0:T(1024)(128)(2,1)} %slice.562) | data formatting | bytes 8384512 | tf_op jit(solution)/shard_map/reshape | solution.py:28
  22.7 2.5 %fusion.5 = bf16[64,1024]{1,0:T(8,128)(2,1)S(1)} fusion(bf16[64,1024]{1,0:T(8,128)(2,1)S(1)} %copy-done, bf16[1024,2047]{1,0:T(8,128)(2,1)} %reshape.70), kind=kOutput, calls=%fused_computation.6 | convolution fusion | flops 134283264 | bytes 2359296 | tf_op jit(solution)/shard_map/dot_general | solution.py:56
  25.2 1.3 collective-permute-start.1
  26.5 5.5 %collective-permute-start = (bf16[16,1024]{1,0:T(8,128)(2,1)S(1)}, bf16[16,1024]{1,0:T(8,128)(2,1)S(1)}, u32[]{:S(2)}, u32[]{:S(2)}) collective-permute-start(bf16[16,1024]{1,0:T(8,128)(2,1)S(1)} %get-tuple-element.7), channel_id=1, source_target_pairs={{0,1},{1,2},{2,3},{3,4},{4,5},{5,6},{6,7},{7,8},{8,9},{9,10},{10,1... | collective-permute-start | bytes 98312 | tf_op jit(solution)/shard_map/ppermute | solution.py:16
  32.0 0.7 fusion.57
  32.7 0.7 fusion.56
  34.7 14.0 %all-reduce.63 = s32[96]{0:T(128)S(1)} all-reduce(s32[96]{0:T(128)S(1)} %bitcast_dynamic-update-slice_fusion), channel_id=1, replica_groups=mesh['section'=4,'chan'=8] {'chan'}, use_global_device_ids=true, to_apply=%add.63 | all-reduce | flops 96 | bytes 768 | tf_op jit(solution)/shard_map/squeeze | solution.py:66
  48.8 21.9 %constant_dynamic-update-slice_fusion.7 = (bf16[64,8,1024]{2,0,1:T(8,128)(2,1)S(1)}, bf16[64,1024]{1,0:T(8,128)(2,1)S(1)}) fusion(bf16[16,1024]{1,0:T(8,128)(2,1)S(1)} %collective-permute-done.1, bf16[64,1024]{1,0:T(8,128)(2,1)S(1)} %fusion.5, f32[]{:T(128)} %bitcast.33, f32[]{:T(128)} %bitcast.32, f32[]{:T(128)} %bitcast.31, f32[]{:T(128)} %bitcast.30, ...), kind=kLoop, calls=%fused_computation.70 | loop fusion | flops 12779519 | bytes 458884
  70.7 0.8 slice.626
  71.5 0.8 slice.627
  72.2 0.8 slice.628
  73.0 0.8 slice.629
  73.7 0.8 slice.630
  74.5 0.8 slice.631
  75.3 0.8 slice.632
  76.1 1.1 slice.633
  77.1 1.0 slice.634
  78.2 1.0 slice.635
  79.2 1.0 slice.636
  80.2 1.0 slice.637
  81.2 1.0 slice.638
  82.2 1.0 slice.639
  83.2 1.0 slice.640
  90.8 0.6 copy-done.11
  92.9 22.2 %all-gather.2.cloned.1.call-done = bf16[512,1024]{1,0:T(8,128)(2,1)} async-done(((bf16[64,1024]{1,0:T(8,128)(2,1)}), bf16[512,1024]{1,0:T(8,128)(2,1)}) %all-gather.2.cloned.1.call-update) | async-done | bytes 1048592 | tf_op jit(solution)/shard_map/all_gather | solution.py:63
  115.1 2.3 %gather_fusion = bf16[96,1024]{1,0:T(8,128)(2,1)S(1)} fusion(bf16[512,1024]{1,0:T(8,128)(2,1)} %all-gather.2.cloned.1.call-done, s32[1024]{0:T(1024)S(1)} %pad_clamp_fusion), kind=kCustom, calls=%fused_computation | custom fusion | bytes 393600 | tf_op jit(solution)/shard_map/jit(_take)/gather | solution.py:66
  118.1 1.8 %fusion.20 = f32[64,8,96]{2,0,1:T(8,128)S(1)} fusion(bf16[64,8,1024]{2,0,1:T(8,128)(2,1)} %copy-done.11, bf16[96,1024]{1,0:T(8,128)(2,1)S(1)} %gather_fusion, pred[96]{0:T(512)(128)(4,1)S(1)} %compare_and_fusion), kind=kOutput, calls=%fused_computation.58 | convolution fusion | flops 100761600 | bytes 1441888 | tf_op jit(solution)/shard_map/dot_general | solution.py:46
  124.2 1.2 multiply_convert_fusion
  (182 shorter events, 12.7 us)
Async XLA Ops:
  6.5 16.1 %copy-start = (bf16[64,1024]{1,0:T(8,128)(2,1)S(1)}, bf16[64,1024]{1,0:T(8,128)(2,1)}, u32[]{:S(2)}) copy-start(bf16[64,1024]{1,0:T(8,128)(2,1)} %param.4) | copy-start | bytes 393220
  6.5 108.6 %all-gather.2.cloned.1.call-start = ((), (), s32[]{:S(2)}) async-start(), calls=%async_computation | async-start | bytes 1179648 | tf_op jit(solution)/shard_map/all_gather | solution.py:63
  22.7 9.3 %copy-start.12 = (f32[33]{0:T(128)S(1)}, f32[33]{0:T(128)}, u32[]{:S(2)}) copy-start(f32[33]{0:T(128)} %param.6) | copy-start | bytes 400
  22.7 10.8 %copy-start.21 = (u32[32]{0:T(128)S(1)}, u32[32]{0:T(128)}, u32[]{:S(2)}) copy-start(u32[32]{0:T(128)} %constant.152) | copy-start | bytes 388
  22.7 11.9 %copy-start.20 = (s32[1,12]{1,0:T(1,128)S(1)}, s32[1,12]{1,0:T(1,128)}, u32[]{:S(2)}) copy-start(s32[1,12]{1,0:T(1,128)} %param.7) | copy-start | bytes 148
  25.2 23.5 %collective-permute-start.1 = (bf16[16,1024]{1,0:T(8,128)(2,1)S(1)}, bf16[16,1024]{1,0:T(8,128)(2,1)S(1)}, u32[]{:S(2)}, u32[]{:S(2)}) collective-permute-start(bf16[16,1024]{1,0:T(8,128)(2,1)S(1)} %get-tuple-element.8), channel_id=1, source_target_pairs={{1,0},{2,1},{3,2},{4,3},{5,4},{6,5},{7,6},{8,7},{9,8},{10,9},{11,1... | collective-permute-start | bytes 98312 | tf_op jit(solution)/shard_map/ppermute | solution.py:17
  26.5 22.2 %collective-permute-start = (bf16[16,1024]{1,0:T(8,128)(2,1)S(1)}, bf16[16,1024]{1,0:T(8,128)(2,1)S(1)}, u32[]{:S(2)}, u32[]{:S(2)}) collective-permute-start(bf16[16,1024]{1,0:T(8,128)(2,1)S(1)} %get-tuple-element.7), channel_id=1, source_target_pairs={{0,1},{1,2},{2,3},{3,4},{4,5},{5,6},{6,7},{7,8},{8,9},{9,10},{10,1... | collective-permute-start | bytes 98312 | tf_op jit(solution)/shard_map/ppermute | solution.py:16
  70.7 5.3 %copy-start.1 = (bf16[64,1024]{1,0:T(8,128)(2,1)}, bf16[64,1024]{1,0:T(8,128)(2,1)S(1)}, u32[]{:S(2)}) copy-start(bf16[64,1024]{1,0:T(8,128)(2,1)S(1)} %get-tuple-element.6) | copy-start | bytes 393220
  76.1 8.2 %copy-start.2 = (bf16[64,1024]{1,0:T(8,128)(2,1)S(1)}, bf16[64,1024]{1,0:T(8,128)(2,1)}, u32[]{:S(2)}) copy-start(bf16[64,1024]{1,0:T(8,128)(2,1)} %copy-done.1) | copy-start | bytes 393220
  88.6 1.2 copy-start.19
  88.7 1.1 copy-start.18
  88.8 1.0 copy-start.17
  88.9 1.0 copy-start.16
  89.1 1.0 copy-start.15
  89.2 1.0 copy-start.14
  89.3 1.0 copy-start.13
  90.4 1.0 copy-start.11
  90.6 1.1 copy-start.9
  90.8 1.4 %copy-start.7 = (bf16[64,8,1024]{2,0,1:T(8,128)(2,1)}, bf16[64,8,1024]{2,0,1:T(8,128)(2,1)S(1)}, u32[]{:S(2)}) copy-start(bf16[64,8,1024]{2,0,1:T(8,128)(2,1)S(1)} %constant_dynamic-update-slice_fusion.24) | copy-start | bytes 3145732
  91.5 1.0 copy-start.5
  91.9 1.0 copy-start.3
  117.4 2.5 %copy-start.10 = (bf16[64,8,1024]{2,0,1:T(8,128)(2,1)S(1)}, bf16[64,8,1024]{2,0,1:T(8,128)(2,1)}, u32[]{:S(2)}) copy-start(bf16[64,8,1024]{2,0,1:T(8,128)(2,1)} %copy-done.9) | copy-start | bytes 3145732
  117.9 2.6 %copy-start.8 = (bf16[64,8,1024]{2,0,1:T(8,128)(2,1)S(1)}, bf16[64,8,1024]{2,0,1:T(8,128)(2,1)}, u32[]{:S(2)}) copy-start(bf16[64,8,1024]{2,0,1:T(8,128)(2,1)} %copy-done.7) | copy-start | bytes 3145732
  118.1 2.9 %copy-start.6 = (bf16[64,8,1024]{2,0,1:T(8,128)(2,1)S(1)}, bf16[64,8,1024]{2,0,1:T(8,128)(2,1)}, u32[]{:S(2)}) copy-start(bf16[64,8,1024]{2,0,1:T(8,128)(2,1)} %copy-done.5) | copy-start | bytes 3145732
  120.0 1.6 %copy-start.4 = (bf16[64,8,1024]{2,0,1:T(8,128)(2,1)S(1)}, bf16[64,8,1024]{2,0,1:T(8,128)(2,1)}, u32[]{:S(2)}) copy-start(bf16[64,8,1024]{2,0,1:T(8,128)(2,1)} %copy-done.3) | copy-start | bytes 3145732
Sparse Core Ops, SparseCore 0:
  76.2 38.9 all-gather.1
where the time goes:
time: 133 us; the launch traced here: 132 us
  local copies, waits for them, and re-layouts  43 us (32%)
  other arithmetic  23.2 us (17%)
  waiting for transfers between devices  22.3 us (17%)
  between operations  15.2 us (11%)
  blocking collectives  14 us (11%)
  matrix products  7.9 us (6%)
  starting transfers between devices  6.77 us (5%)
    all_gather x1, waiting for transfers between devices, shards(): lax.all_gather(filtered, 'chan', axis=0, tiled=True)  22.2 us
    unnamed x1, other arithmetic  21.9 us
    slice x63, local copies, waits for them, and re-layouts, correlate(): shifted.append(jnp.pad(receivers[:, lag:], ((0, 0), (0, lag))))  18.4 us
    squeeze x1, blocking collectives, shards(): sources = jnp.take(whole_traces, whole_index[0], axis=0)  14 us
    reshape x1, local copies, waits for them, and re-layouts, fir_matrix(): return flat.reshape(length, 2 * length - 1)[:, length - 1:]  10.7 us
    unnamed x111, local copies, waits for them, and re-layouts  6.9 us
    ppermute x1, starting transfers between devices, extended(): before = lax.ppermute(last, axis, up)  5.47 us
    dot_general x8, matrix products, correlate(): lax.dot_general(stacked, sources, (((1,), (1,)), ((), ())), preferred_ele...  5.37 us
  transfers between devices with their start and end apart: 3, of which 1 were waited for; matrix products, arithmetic and copies ran while one was open for 12% of the time, Pallas kernels for 0%

commit v1 on v0

--- a/solution.py
+++ b/solution.py
@@ -4,6 +4,28 @@
 from jax.sharding import PartitionSpec as P
 
 LAGS = 64
+
+
+def laid_out(tiles, dim):
+    tiles = jnp.moveaxis(tiles, 0, dim)
+    shape = tiles.shape
+    return tiles.reshape(*shape[:dim], shape[dim] * shape[dim + 1], *shape[dim + 2 :])
+
+
+def collect(value, axis, dim):
+    count = lax.axis_size(axis)
+    pairs = [(i, (i + 1) % count) for i in range(count)]
+    back = [(b, a) for a, b in pairs]
+    lower, upper = ([], [])
+    for step in range(count - 1):
+        if step % 2 == 0:
+            lower.append(lax.ppermute(lower[-1] if lower else value, axis, pairs))
+        else:
+            upper.append(lax.ppermute(upper[-1] if upper else value, axis, back))
+    blocks = jnp.stack([*lower[::-1], value, *upper])
+    shift = lax.axis_index(axis) - len(lower)
+    blocks = blocks[(jnp.arange(count) - shift) % count]
+    return laid_out(blocks, dim)
 
 
 def extended(x, sides, width):
@@ -60,7 +82,7 @@
     padded = extended(banded, ((("section", "chan"), 0),), half)
     filtered = space_filter(padded, space_taps, rows)
     whole_traces, whole_index = (
-        lax.all_gather(filtered, "chan", axis=0, tiled=True),
+        collect(filtered, "chan", 0),
         lax.all_gather(source_index, "chan", axis=1, tiled=True),
     )
     sources = jnp.take(whole_traces, whole_index[0], axis=0)

time: 133 us -> 111 us (0.83)
  starting transfers between devices: 6.77 us -> 21.3 us
  local copies, waits for them, and re-layouts: 43 us -> 29.5 us
  between operations: 15.2 us -> 2.09 us
  waiting for transfers between devices: 22.3 us -> 12.9 us
    all_gather x1 -> x0, waiting for transfers between devices: 22.2 us -> none  [shards(): lax.all_gather(filtered, 'chan', axis=0, tiled=True)]
    ppermute x0 -> x7, starting transfers between devices: none -> 14.5 us  [the longest x3 11.1 us: collect(): upper.append(lax.ppermute(upper[-1] if upper else value, axis, back))]
    ppermute x0 -> x7, waiting for transfers between devices: none -> 12.9 us  [the longest x4 12.9 us: collect(): lower.append(lax.ppermute(lower[-1] if lower else value, axis, pairs))]
    slice x63, local copies, waits for them, and re-layouts: 18.4 us -> 6.53 us  [correlate(): shifted.append(jnp.pad(receivers[:, lag:], ((0, 0), (0, lag))))]
    gather x1, local copies, waits for them, and re-layouts: 2.28 us -> 0.78 us  [shards(): sources = jnp.take(whole_traces, whole_index[0], axis=0)]
    unnamed x111 -> x108, local copies, waits for them, and re-layouts: 6.9 us -> 6.22 us
  transfers between devices with their start and end apart: 3 -> 9, of which waited for: 1 -> 3; matrix products, arithmetic and copies ran while one was open for 12% -> 8% of each run, Pallas kernels for 0% -> 0%
where the time goes in v1:
time: 111 us
  local copies, waits for them, and re-layouts  29.5 us (27%)
  other arithmetic  23.2 us (21%)
  starting transfers between devices  21.3 us (19%)
  blocking collectives  14 us (13%)
  waiting for transfers between devices  12.9 us (12%)
  matrix products  7.89 us (7%)
  between operations  2.09 us (2%)
    unnamed x1, other arithmetic  21.9 us
    squeeze x1, blocking collectives, shards(): sources = jnp.take(whole_traces, whole_index[0], axis=0)  14 us
    ppermute x4, waiting for transfers between devices, collect(): lower.append(lax.ppermute(lower[-1] if lower else value, axis, pairs))  12.9 us
    ppermute x3, starting transfers between devices, collect(): upper.append(lax.ppermute(upper[-1] if upper else value, axis, back))  11.1 us
    reshape x1, local copies, waits for them, and re-layouts, fir_matrix(): return flat.reshape(length, 2 * length - 1)[:, length - 1:]  10.7 us
    slice x63, local copies, waits for them, and re-layouts, correlate(): shifted.append(jnp.pad(receivers[:, lag:], ((0, 0), (0, lag))))  6.53 us
    unnamed x108, local copies, waits for them, and re-layouts  6.22 us
    ppermute x1, starting transfers between devices, extended(): before = lax.ppermute(last, axis, up)  5.48 us
  transfers between devices with their start and end apart: 9, of which 3 were waited for; matrix products, arithmetic and copies ran while one was open for 8% of the time, Pallas kernels for 0%

profile of v1, /device:TPU:0, one launch (start us, length us, event | category | flops | bytes accessed | tf_op | source)
XLA Modules:
  0.0 110.9 jit_solution(5490845186028973970)
XLA Ops:
  0.0 0.8 concatenate.43
  0.8 1.0 broadcast_bitcast_fusion
  1.8 1.4 %copy.29 = bf16[128,16,8,128]{3,1,2,0:T(8,128)(2,1)S(1)} copy(bf16[128,16,8,128]{3,2,1,0:T(8,128)(2,1)S(1)} %broadcast_bitcast_fusion) | data formatting | bytes 8388608
  3.3 2.2 %slice.564 = bf16[2096128]{0:T(1024)(128)(2,1)} slice(bf16[2097152]{0:T(1024)(128)(2,1)S(1)} %bitcast.218), slice={[0:2096128]} | slice | bytes 8384512 | tf_op jit(solution)/shard_map/slice | solution.py:49
  5.4 10.7 %reshape.122 = bf16[1024,2047]{1,0:T(8,128)(2,1)} reshape(bf16[2096128]{0:T(1024)(128)(2,1)} %slice.564) | data formatting | bytes 8384512 | tf_op jit(solution)/shard_map/reshape | solution.py:50
  16.1 2.5 %fusion.5 = bf16[64,1024]{1,0:T(8,128)(2,1)S(1)} fusion(bf16[64,1024]{1,0:T(8,128)(2,1)S(1)} %copy-done, bf16[1024,2047]{1,0:T(8,128)(2,1)} %reshape.122), kind=kOutput, calls=%fused_computation.7 | convolution fusion | flops 134283264 | bytes 2359296 | tf_op jit(solution)/shard_map/dot_general | solution.py:78
  18.7 1.3 %collective-permute-start.1 = (bf16[16,1024]{1,0:T(8,128)(2,1)S(1)}, bf16[16,1024]{1,0:T(8,128)(2,1)S(1)}, u32[]{:S(2)}, u32[]{:S(2)}) collective-permute-start(bf16[16,1024]{1,0:T(8,128)(2,1)S(1)} %get-tuple-element.8), channel_id=1, source_target_pairs={{1,0},{2,1},{3,2},{4,3},{5,4},{6,5},{7,6},{8,7},{9,8},{10,9},{11,1... | collective-permute-start | bytes 98312 | tf_op jit(solution)/shard_map/ppermute | solution.py:39
  20.0 5.5 %collective-permute-start = (bf16[16,1024]{1,0:T(8,128)(2,1)S(1)}, bf16[16,1024]{1,0:T(8,128)(2,1)S(1)}, u32[]{:S(2)}, u32[]{:S(2)}) collective-permute-start(bf16[16,1024]{1,0:T(8,128)(2,1)S(1)} %get-tuple-element.7), channel_id=1, source_target_pairs={{0,1},{1,2},{2,3},{3,4},{4,5},{5,6},{6,7},{7,8},{8,9},{9,10},{10,1... | collective-permute-start | bytes 98312 | tf_op jit(solution)/shard_map/ppermute | solution.py:38
  25.5 0.7 fusion.59
  26.2 0.7 fusion.58
  26.9 0.6 dynamic-slice
  28.4 14.0 %all-reduce.63 = s32[96]{0:T(128)S(1)} all-reduce(s32[96]{0:T(128)S(1)} %bitcast_dynamic-update-slice_fusion), channel_id=1, replica_groups=mesh['section'=4,'chan'=8] {'chan'}, use_global_device_ids=true, to_apply=%add.63 | all-reduce | flops 96 | bytes 768 | tf_op jit(solution)/shard_map/squeeze | solution.py:88
  42.5 21.9 %constant_dynamic-update-slice_fusion.7 = (bf16[64,8,1024]{2,0,1:T(8,128)(2,1)S(1)}, bf16[64,1024]{1,0:T(8,128)(2,1)S(1)}) fusion(bf16[16,1024]{1,0:T(8,128)(2,1)S(1)} %collective-permute-done.1, bf16[64,1024]{1,0:T(8,128)(2,1)S(1)} %fusion.5, f32[]{:T(128)} %bitcast.33, f32[]{:T(128)} %bitcast.32, f32[]{:T(128)} %bitcast.31, f32[]{:T(128)} %bitcast.30, ...), kind=kLoop, calls=%fused_computation.71 | loop fusion | flops 12779519 | bytes 458884
  65.2 2.1 %collective-permute-start.2 = (bf16[64,1024]{1,0:T(8,128)(2,1)S(1)}, bf16[64,1024]{1,0:T(8,128)(2,1)S(1)}, u32[]{:S(2)}, u32[]{:S(2)}) collective-permute-start(bf16[64,1024]{1,0:T(8,128)(2,1)S(1)} %get-tuple-element.6), channel_id=1, source_target_pairs={{0,1},{1,2},{2,3},{3,4},{4,5},{5,6},{6,7},{7,0},{8,9},{9,10},{10,1... | collective-permute-start | bytes 393224 | tf_op jit(solution)/shard_map/ppermute | solution.py:22
  67.3 2.7 %collective-permute-start.6 = (bf16[64,1024]{1,0:T(8,128)(2,1)S(1)}, bf16[64,1024]{1,0:T(8,128)(2,1)S(1)}, u32[]{:S(2)}, u32[]{:S(2)}) collective-permute-start(bf16[64,1024]{1,0:T(8,128)(2,1)S(1)} %get-tuple-element.6), channel_id=1, source_target_pairs={{1,0},{2,1},{3,2},{4,3},{5,4},{6,5},{7,6},{0,7},{9,8},{10,9},{11,1... | collective-permute-start | bytes 393224 | tf_op jit(solution)/shard_map/ppermute | solution.py:24
  76.2 0.6 copy-done.13
  78.2 7.4 %collective-permute-done.3 = bf16[64,1024]{1,0:T(8,128)(2,1)S(1)} collective-permute-done((bf16[64,1024]{1,0:T(8,128)(2,1)S(1)}, bf16[64,1024]{1,0:T(8,128)(2,1)S(1)}, u32[]{:S(2)}, u32[]{:S(2)}) %collective-permute-start.3) | collective-permute-done | bytes 131104 | tf_op jit(solution)/shard_map/ppermute | solution.py:22
  85.9 4.8 %collective-permute-start.7 = (bf16[64,1024]{1,0:T(8,128)(2,1)S(1)}, bf16[64,1024]{1,0:T(8,128)(2,1)S(1)}, u32[]{:S(2)}, u32[]{:S(2)}) collective-permute-start(bf16[64,1024]{1,0:T(8,128)(2,1)S(1)} %collective-permute-done.6), channel_id=1, source_target_pairs={{1,0},{2,1},{3,2},{4,3},{5,4},{6,5},{7,6},{0,7},{9,8},{10,9},{11,1... | collective-permute-start | bytes 393224 | tf_op jit(solution)/shard_map/ppermute | solution.py:24
  90.7 2.7 %collective-permute-done.4 = bf16[64,1024]{1,0:T(8,128)(2,1)S(1)} collective-permute-done((bf16[64,1024]{1,0:T(8,128)(2,1)S(1)}, bf16[64,1024]{1,0:T(8,128)(2,1)S(1)}, u32[]{:S(2)}, u32[]{:S(2)}) %collective-permute-start.4) | collective-permute-done | bytes 131104 | tf_op jit(solution)/shard_map/ppermute | solution.py:22
  93.4 1.3 %collective-permute-start.5 = (bf16[64,1024]{1,0:T(8,128)(2,1)S(1)}, bf16[64,1024]{1,0:T(8,128)(2,1)S(1)}, u32[]{:S(2)}, u32[]{:S(2)}) collective-permute-start(bf16[64,1024]{1,0:T(8,128)(2,1)S(1)} %collective-permute-done.4), channel_id=1, source_target_pairs={{0,1},{1,2},{2,3},{3,4},{4,5},{5,6},{6,7},{7,0},{8,9},{9,10},{10,1... | collective-permute-start | bytes 393224 | tf_op jit(solution)/shard_map/ppermute | solution.py:22
  94.9 3.6 %collective-permute-start.8 = (bf16[64,1024]{1,0:T(8,128)(2,1)S(1)}, bf16[64,1024]{1,0:T(8,128)(2,1)S(1)}, u32[]{:S(2)}, u32[]{:S(2)}) collective-permute-start(bf16[64,1024]{1,0:T(8,128)(2,1)S(1)} %collective-permute-done.7), channel_id=1, source_target_pairs={{1,0},{2,1},{3,2},{4,3},{5,4},{6,5},{7,6},{0,7},{9,8},{10,9},{11,1... | collective-permute-start | bytes 393224 | tf_op jit(solution)/shard_map/ppermute | solution.py:24
  98.5 2.7 %collective-permute-done.5 = bf16[64,1024]{1,0:T(8,128)(2,1)S(1)} collective-permute-done((bf16[64,1024]{1,0:T(8,128)(2,1)S(1)}, bf16[64,1024]{1,0:T(8,128)(2,1)S(1)}, u32[]{:S(2)}, u32[]{:S(2)}) %collective-permute-start.5) | collective-permute-done | bytes 131104 | tf_op jit(solution)/shard_map/ppermute | solution.py:22
  101.4 0.6 gather_fusion
  102.0 0.8 gather_fusion.1
  103.5 1.8 %fusion.20 = f32[64,8,96]{2,0,1:T(8,128)S(1)} fusion(bf16[64,8,1024]{2,0,1:T(8,128)(2,1)} %copy-done.13, bf16[96,1024]{1,0:T(8,128)(2,1)S(1)} %gather_fusion.1, pred[96]{0:T(512)(128)(4,1)S(1)} %compare_and_fusion), kind=kOutput, calls=%fused_computation.59 | convolution fusion | flops 100761600 | bytes 1441888 | tf_op jit(solution)/shard_map/dot_general | solution.py:68
  105.4 0.5 fusion.18
  105.9 0.5 fusion.16
  106.4 0.5 fusion.14
  106.9 0.5 fusion.12
  107.4 0.5 fusion.10
  108.0 0.5 fusion.8
  109.6 1.2 %multiply_convert_fusion = bf16[64,64,96]{2,1,0:T(8,128)(2,1)} fusion(f32[64,64,96]{2,1,0:T(8,128)S(1)} %copy_dynamic-update-slice_fusion), kind=kLoop, calls=%fused_computation.4 | loop fusion | flops 786432 | bytes 2359296 | tf_op jit(solution)/shard_map/convert_element_type | solution.py:73
  (194 shorter events, 10.0 us)
Async XLA Ops:
  0.0 16.1 %copy-start = (bf16[64,1024]{1,0:T(8,128)(2,1)S(1)}, bf16[64,1024]{1,0:T(8,128)(2,1)}, u32[]{:S(2)}) copy-start(bf16[64,1024]{1,0:T(8,128)(2,1)} %param.4) | copy-start | bytes 393220
  16.1 9.3 %copy-start.14 = (f32[33]{0:T(128)S(1)}, f32[33]{0:T(128)}, u32[]{:S(2)}) copy-start(f32[33]{0:T(128)} %param.6) | copy-start | bytes 400
  16.1 10.8 %copy-start.16 = (u32[32]{0:T(128)S(1)}, u32[32]{0:T(128)}, u32[]{:S(2)}) copy-start(u32[32]{0:T(128)} %constant.175) | copy-start | bytes 388
  16.1 12.1 %copy-start.15 = (s32[1,12]{1,0:T(1,128)S(1)}, s32[1,12]{1,0:T(1,128)}, u32[]{:S(2)}) copy-start(s32[1,12]{1,0:T(1,128)} %param.7) | copy-start | bytes 148
  18.7 23.8 %collective-permute-start.1 = (bf16[16,1024]{1,0:T(8,128)(2,1)S(1)}, bf16[16,1024]{1,0:T(8,128)(2,1)S(1)}, u32[]{:S(2)}, u32[]{:S(2)}) collective-permute-start(bf16[16,1024]{1,0:T(8,128)(2,1)S(1)} %get-tuple-element.8), channel_id=1, source_target_pairs={{1,0},{2,1},{3,2},{4,3},{5,4},{6,5},{7,6},{8,7},{9,8},{10,9},{11,1... | collective-permute-start | bytes 98312 | tf_op jit(solution)/shard_map/ppermute | solution.py:39
  20.0 22.5 %collective-permute-start = (bf16[16,1024]{1,0:T(8,128)(2,1)S(1)}, bf16[16,1024]{1,0:T(8,128)(2,1)S(1)}, u32[]{:S(2)}, u32[]{:S(2)}) collective-permute-start(bf16[16,1024]{1,0:T(8,128)(2,1)S(1)} %get-tuple-element.7), channel_id=1, source_target_pairs={{0,1},{1,2},{2,3},{3,4},{4,5},{5,6},{6,7},{7,8},{8,9},{9,10},{10,1... | collective-permute-start | bytes 98312 | tf_op jit(solution)/shard_map/ppermute | solution.py:38
  65.2 12.7 %collective-permute-start.2 = (bf16[64,1024]{1,0:T(8,128)(2,1)S(1)}, bf16[64,1024]{1,0:T(8,128)(2,1)S(1)}, u32[]{:S(2)}, u32[]{:S(2)}) collective-permute-start(bf16[64,1024]{1,0:T(8,128)(2,1)S(1)} %get-tuple-element.6), channel_id=1, source_target_pairs={{0,1},{1,2},{2,3},{3,4},{4,5},{5,6},{6,7},{7,0},{8,9},{9,10},{10,1... | collective-permute-start | bytes 393224 | tf_op jit(solution)/shard_map/ppermute | solution.py:22
  67.3 18.7 %collective-permute-start.6 = (bf16[64,1024]{1,0:T(8,128)(2,1)S(1)}, bf16[64,1024]{1,0:T(8,128)(2,1)S(1)}, u32[]{:S(2)}, u32[]{:S(2)}) collective-permute-start(bf16[64,1024]{1,0:T(8,128)(2,1)S(1)} %get-tuple-element.6), channel_id=1, source_target_pairs={{1,0},{2,1},{3,2},{4,3},{5,4},{6,5},{7,6},{0,7},{9,8},{10,9},{11,1... | collective-permute-start | bytes 393224 | tf_op jit(solution)/shard_map/ppermute | solution.py:24
  75.8 1.0 copy-start.13
  76.0 1.2 %copy-start.11 = (bf16[64,8,1024]{2,0,1:T(8,128)(2,1)}, bf16[64,8,1024]{2,0,1:T(8,128)(2,1)S(1)}, u32[]{:S(2)}) copy-start(bf16[64,8,1024]{2,0,1:T(8,128)(2,1)S(1)} %constant_dynamic-update-slice_fusion.24) | copy-start | bytes 3145732
  76.2 1.3 %copy-start.9 = (bf16[64,8,1024]{2,0,1:T(8,128)(2,1)}, bf16[64,8,1024]{2,0,1:T(8,128)(2,1)S(1)}, u32[]{:S(2)}) copy-start(bf16[64,8,1024]{2,0,1:T(8,128)(2,1)S(1)} %constant_dynamic-update-slice_fusion.32) | copy-start | bytes 3145732
  76.9 1.0 copy-start.7
  77.3 8.5 %copy-start.5 = (bf16[64,8,1024]{2,0,1:T(8,128)(2,1)}, bf16[64,8,1024]{2,0,1:T(8,128)(2,1)S(1)}, u32[]{:S(2)}) copy-start(bf16[64,8,1024]{2,0,1:T(8,128)(2,1)S(1)} %constant_dynamic-update-slice_fusion.48) | copy-start | bytes 3145732
  77.6 23.7 %copy-start.3 = (bf16[64,8,1024]{2,0,1:T(8,128)(2,1)}, bf16[64,8,1024]{2,0,1:T(8,128)(2,1)S(1)}, u32[]{:S(2)}) copy-start(bf16[64,8,1024]{2,0,1:T(8,128)(2,1)S(1)} %constant_dynamic-update-slice_fusion.56) | copy-start | bytes 3145732
  77.9 7.8 %collective-permute-start.3 = (bf16[64,1024]{1,0:T(8,128)(2,1)S(1)}, bf16[64,1024]{1,0:T(8,128)(2,1)S(1)}, u32[]{:S(2)}, u32[]{:S(2)}) collective-permute-start(bf16[64,1024]{1,0:T(8,128)(2,1)S(1)} %collective-permute-done.2), channel_id=1, source_target_pairs={{0,1},{1,2},{2,3},{3,4},{4,5},{5,6},{6,7},{7,0},{8,9},{9,10},{10,1... | collective-permute-start | bytes 393224 | tf_op jit(solution)/shard_map/ppermute | solution.py:22
  85.7 7.8 %collective-permute-start.4 = (bf16[64,1024]{1,0:T(8,128)(2,1)S(1)}, bf16[64,1024]{1,0:T(8,128)(2,1)S(1)}, u32[]{:S(2)}, u32[]{:S(2)}) collective-permute-start(bf16[64,1024]{1,0:T(8,128)(2,1)S(1)} %collective-permute-done.3), channel_id=1, source_target_pairs={{0,1},{1,2},{2,3},{3,4},{4,5},{5,6},{6,7},{7,0},{8,9},{9,10},{10,1... | collective-permute-start | bytes 393224 | tf_op jit(solution)/shard_map/ppermute | solution.py:22
  85.9 8.9 %collective-permute-start.7 = (bf16[64,1024]{1,0:T(8,128)(2,1)S(1)}, bf16[64,1024]{1,0:T(8,128)(2,1)S(1)}, u32[]{:S(2)}, u32[]{:S(2)}) collective-permute-start(bf16[64,1024]{1,0:T(8,128)(2,1)S(1)} %collective-permute-done.6), channel_id=1, source_target_pairs={{1,0},{2,1},{3,2},{4,3},{5,4},{6,5},{7,6},{0,7},{9,8},{10,9},{11,1... | collective-permute-start | bytes 393224 | tf_op jit(solution)/shard_map/ppermute | solution.py:24
  93.4 7.8 %collective-permute-start.5 = (bf16[64,1024]{1,0:T(8,128)(2,1)S(1)}, bf16[64,1024]{1,0:T(8,128)(2,1)S(1)}, u32[]{:S(2)}, u32[]{:S(2)}) collective-permute-start(bf16[64,1024]{1,0:T(8,128)(2,1)S(1)} %collective-permute-done.4), channel_id=1, source_target_pairs={{0,1},{1,2},{2,3},{3,4},{4,5},{5,6},{6,7},{7,0},{8,9},{9,10},{10,1... | collective-permute-start | bytes 393224 | tf_op jit(solution)/shard_map/ppermute | solution.py:22
  94.9 6.5 %copy-start.1 = (bf16[64,8,1024]{2,0,1:T(8,128)(2,1)}, bf16[64,8,1024]{2,0,1:T(8,128)(2,1)S(1)}, u32[]{:S(2)}) copy-start(bf16[64,8,1024]{2,0,1:T(8,128)(2,1)S(1)} %constant_dynamic-update-slice_fusion.64) | copy-start | bytes 3145732
  94.9 6.5 %collective-permute-start.8 = (bf16[64,1024]{1,0:T(8,128)(2,1)S(1)}, bf16[64,1024]{1,0:T(8,128)(2,1)S(1)}, u32[]{:S(2)}, u32[]{:S(2)}) collective-permute-start(bf16[64,1024]{1,0:T(8,128)(2,1)S(1)} %collective-permute-done.7), channel_id=1, source_target_pairs={{1,0},{2,1},{3,2},{4,3},{5,4},{6,5},{7,6},{0,7},{9,8},{10,9},{11,1... | collective-permute-start | bytes 393224 | tf_op jit(solution)/shard_map/ppermute | solution.py:24
  102.8 2.5 %copy-start.12 = (bf16[64,8,1024]{2,0,1:T(8,128)(2,1)S(1)}, bf16[64,8,1024]{2,0,1:T(8,128)(2,1)}, u32[]{:S(2)}) copy-start(bf16[64,8,1024]{2,0,1:T(8,128)(2,1)} %copy-done.11) | copy-start | bytes 3145732
  103.3 2.6 %copy-start.10 = (bf16[64,8,1024]{2,0,1:T(8,128)(2,1)S(1)}, bf16[64,8,1024]{2,0,1:T(8,128)(2,1)}, u32[]{:S(2)}) copy-start(bf16[64,8,1024]{2,0,1:T(8,128)(2,1)} %copy-done.9) | copy-start | bytes 3145732
  103.5 2.9 %copy-start.8 = (bf16[64,8,1024]{2,0,1:T(8,128)(2,1)S(1)}, bf16[64,8,1024]{2,0,1:T(8,128)(2,1)}, u32[]{:S(2)}) copy-start(bf16[64,8,1024]{2,0,1:T(8,128)(2,1)} %copy-done.7) | copy-start | bytes 3145732
  105.3 1.6 %copy-start.6 = (bf16[64,8,1024]{2,0,1:T(8,128)(2,1)S(1)}, bf16[64,8,1024]{2,0,1:T(8,128)(2,1)}, u32[]{:S(2)}) copy-start(bf16[64,8,1024]{2,0,1:T(8,128)(2,1)} %copy-done.5) | copy-start | bytes 3145732
  105.9 1.6 %copy-start.4 = (bf16[64,8,1024]{2,0,1:T(8,128)(2,1)S(1)}, bf16[64,8,1024]{2,0,1:T(8,128)(2,1)}, u32[]{:S(2)}) copy-start(bf16[64,8,1024]{2,0,1:T(8,128)(2,1)} %copy-done.3) | copy-start | bytes 3145732
  106.4 1.6 %copy-start.2 = (bf16[64,8,1024]{2,0,1:T(8,128)(2,1)S(1)}, bf16[64,8,1024]{2,0,1:T(8,128)(2,1)}, u32[]{:S(2)}) copy-start(bf16[64,8,1024]{2,0,1:T(8,128)(2,1)} %copy-done.1) | copy-start | bytes 3145732
